TPU v7x, 32 devices: a whole 2x2x4 slice. The times are simulated.
32 devices in a mesh: outer: 4 (over x, core), inner: 8 (over z, y).
Axes of the slice: x: 2, y: 2, z: 4, core: 2. Of those that a mesh axis runs over, the one named last changes fastest.
Arguments:
- signal: bfloat16 [4096, 4096], P(('outer', 'inner')), may hold values from -6 to 6
- gating: bfloat16 [4096, 4096], P(('outer', 'inner')), may hold values from -6 to 6
- decay_rate: float32 [4096, 16], P('inner'), may hold values from 0.00012207031 to 0.05
- residues: float32 [4096, 16], P('inner'), may hold values from -1.5 to 1.5
- skip_gain: float32 [4096], replicated, may hold values from -3 to 3
Outputs:
- layer_out: bfloat16 [4096, 4096], P(('outer', 'inner'))
All inputs are finite; a program needn't handle non-finite values.
Results may differ from a plain program's by a relative error of at most 0.001.
Values may be sent and summed in bfloat16 or wider, within the bound.
A program may use at most 128 MiB of HBM per device.

v0:
```python
import math

import jax
import jax.numpy as jnp
from jax import lax
from jax.sharding import PartitionSpec as P


def filter_spectrum(frequency, padded, seq_length, decay_rate, residues):
    angles = frequency.astype(jnp.float32) * (2.0 * math.pi / padded)
    sine_half = jnp.sin(0.5 * angles)
    bending = 2.0 * sine_half * sine_half
    sine_full = jnp.sin(angles)
    parity = (1 - 2 * (frequency % 2)).astype(jnp.float32)
    zeros_out = jnp.zeros_like(angles + decay_rate[:, 0])

    def add_mode(mode_index, totals):
        real_sum, imag_sum = totals
        mode_rate = lax.dynamic_index_in_dim(decay_rate, mode_index, 1, keepdims=False)
        weights = lax.dynamic_index_in_dim(residues, mode_index, 1, keepdims=False)
        decays = jnp.exp(-mode_rate)
        scaled = weights * jnp.sqrt(-jnp.expm1(-2.0 * mode_rate))
        numerator = scaled * (1.0 - jnp.exp(-seq_length * mode_rate) * parity)
        den_real = -jnp.expm1(-mode_rate) + decays * bending
        den_imag = decays * sine_full
        quotient = numerator / (den_real * den_real + den_imag * den_imag)
        return (real_sum + quotient * den_real, imag_sum - quotient * den_imag)

    return lax.fori_loop(0, decay_rate.shape[1], add_mode, (zeros_out, zeros_out))


def dft_pair(length_n, direction):
    index_range = jnp.arange(length_n, dtype=jnp.int32)
    phases = index_range[:, None] * index_range[None, :] % length_n
    angles = phases.astype(jnp.float32) * (direction * 2.0 * math.pi / length_n)
    return (jnp.cos(angles), jnp.sin(angles))


def complex_apply(pattern, matrix_pair, real_in, imag_in):
    matrix_re, matrix_im = matrix_pair

    def product(left, right):
        return jnp.einsum(pattern, left, right, precision=lax.Precision.HIGHEST)

    real_out = product(matrix_re, real_in) - product(matrix_im, imag_in)
    imag_out = product(matrix_re, imag_in) + product(matrix_im, real_in)
    return (real_out, imag_out)


def rotate(real_in, imag_in, angles):
    cosine = jnp.cos(angles)
    sine = jnp.sin(angles)
    return (cosine * real_in - sine * imag_in, sine * real_in + cosine * imag_in)


def outer_terms(block_piece, block_rows, group_index, groups):
    piece_rows = block_piece.shape[0]
    owners = jnp.arange(piece_rows, dtype=jnp.int32) // block_rows
    kept_freq = jnp.arange(2, dtype=jnp.int32) * groups + group_index
    phases = kept_freq[:, None] * owners[None, :] % (2 * groups)
    angles = phases.astype(jnp.float32) * (-math.pi / groups)
    trailing = (1,) * (block_piece.ndim - 1)
    angles = angles.reshape((2, piece_rows) + trailing)
    values_f = block_piece.astype(jnp.float32)[None]
    return jnp.stack([jnp.cos(angles) * values_f, jnp.sin(angles) * values_f])


def inverse_terms(real_w, imag_w, row_count, block_rows, group_index, groups, padded):
    owner_count = row_count // block_rows
    owners = jnp.arange(owner_count, dtype=jnp.int32)
    phases = owners * group_index % (2 * groups)
    angles = phases.astype(jnp.float32) * (math.pi / groups)
    parity = (1 - 2 * (owners % 2)).astype(jnp.float32)
    trailing = (1,) * (real_w.ndim - 1)
    angles = angles.reshape((owner_count,) + trailing)
    parity = parity.reshape((owner_count,) + trailing)
    summed_re = real_w[0][None] + parity * real_w[1][None]
    summed_im = imag_w[0][None] + parity * imag_w[1][None]
    terms = (jnp.cos(angles) * summed_re - jnp.sin(angles) * summed_im) * (1.0 / padded)
    return terms.reshape((row_count,) + real_w.shape[2:])


def spectral_core(real_part, imag_part, group_index, groups, decay_rate, residues):
    lane_count = real_part.shape[1]
    tok_rows = real_part.shape[2]
    points = groups * lane_count
    padded = 2 * points * tok_rows
    kept_freq = jnp.arange(2, dtype=jnp.int32) * groups + group_index
    lane_index = jnp.arange(lane_count, dtype=jnp.int32)
    row_index = jnp.arange(tok_rows, dtype=jnp.int32)
    lane_phase = (kept_freq[:, None] * lane_index[None, :] % (2 * points)).astype(jnp.float32)
    lane_angle = (lane_phase * (-math.pi / points))[:, :, None, None]
    real_part, imag_part = rotate(real_part, imag_part, lane_angle)
    real_part, imag_part = complex_apply(
        "vi,qibc->qvbc", dft_pair(lane_count, -1.0), real_part, imag_part
    )
    coarse = kept_freq[:, None] + 2 * groups * lane_index[None, :]
    fine_phase = (coarse[:, :, None] * row_index[None, None, :] % padded).astype(jnp.float32)
    fine_angle = (fine_phase * (-2.0 * math.pi / padded))[..., None]
    real_part, imag_part = rotate(real_part, imag_part, fine_angle)
    real_part, imag_part = complex_apply(
        "db,qvbc->qvdc", dft_pair(tok_rows, -1.0), real_part, imag_part
    )
    frequency = (coarse[:, :, None] + 2 * points * row_index[None, None, :])[..., None]
    filter_re, filter_im = filter_spectrum(
        frequency, padded, points * tok_rows, decay_rate, residues
    )
    real_part, imag_part = (
        real_part * filter_re - imag_part * filter_im,
        real_part * filter_im + imag_part * filter_re,
    )
    real_part, imag_part = complex_apply(
        "bd,qvdc->qvbc", dft_pair(tok_rows, 1.0), real_part, imag_part
    )
    real_part, imag_part = rotate(real_part, imag_part, -fine_angle)
    real_part, imag_part = complex_apply(
        "iv,qvbc->qibc", dft_pair(lane_count, 1.0), real_part, imag_part
    )
    return rotate(real_part, imag_part, -lane_angle)


def per_device(signal, gating, decay_rate, residues, skip_gain):
    groups = lax.axis_size("outer")
    lane_count = lax.axis_size("inner")
    group_index = lax.axis_index("outer")
    tok_rows, channels = signal.shape
    padded = 2 * groups * lane_count * tok_rows
    weighted = outer_terms(
        lax.all_gather(signal, "outer", axis=0, tiled=True), tok_rows, group_index, groups
    )
    summed = weighted.reshape(2, 2, groups, tok_rows, channels).sum(axis=2)
    real_part, imag_part = (
        lax.all_to_all(summed[0][:, None], "inner", split_axis=3, concat_axis=1, tiled=True),
        lax.all_to_all(summed[1][:, None], "inner", split_axis=3, concat_axis=1, tiled=True),
    )
    real_w, imag_w = spectral_core(real_part, imag_part, group_index, groups, decay_rate, residues)
    real_w, imag_w = (
        lax.all_to_all(real_w, "inner", split_axis=1, concat_axis=3, tiled=True),
        lax.all_to_all(imag_w, "inner", split_axis=1, concat_axis=3, tiled=True),
    )
    real_w = real_w[:, 0]
    imag_w = imag_w[:, 0]
    convolved = lax.psum_scatter(
        inverse_terms(
            real_w, imag_w, tok_rows * lax.axis_size("outer"), tok_rows, group_index, groups, padded
        ),
        "outer",
        scatter_dimension=0,
        tiled=True,
    )
    signal_f = signal.astype(jnp.float32)
    return (gating.astype(jnp.float32) * (convolved + skip_gain[None, :] * signal_f)).astype(
        jnp.bfloat16
    )


def solution(mesh):
    return jax.shard_map(
        per_device,
        mesh=mesh,
        in_specs=(
            P(("outer", "inner"), None),
            P(("outer", "inner"), None),
            P("inner", None),
            P("inner", None),
            P(),
        ),
        out_specs=P(("outer", "inner"), None),
        check_vma=False,
    )
```

profile of v0, /device:TPU:0, one launch (start us, length us, event | category | flops | bytes accessed | tf_op | source)
XLA Modules:
  0.0 760.6 jit_solution(7480544865522417398)
XLA Ops:
  7.4 38.7 %all-gather.2.cloned.1.call-done = bf16[512,4096]{1,0:T(8,128)(2,1)} async-done(((bf16[128,4096]{1,0:T(8,128)(2,1)}), bf16[512,4096]{1,0:T(8,128)(2,1)}) %all-gather.2.cloned.1.call-update) | async-done | bytes 4194320 | tf_op jit(solution)/shard_map/all_gather | solution.py:129
  49.4 11.8 %broadcast_multiply_fusion.1 = (f32[1,2,4,128,4096]{4,3,2,1,0:T(8,128)}, f32[1,2,4,128,4096]{4,3,2,1,0:T(8,128)}) fusion(f32[4,128,4096]{2,1,0:T(8,128)S(1)} %convert.1, f32[2,4,128]{2,1,0:T(4,128)S(1)} %get-tuple-element.274, f32[2,4,128]{2,1,0:T(4,128)S(1)} %get-tuple-element.275), kind=kLoop, calls=%fused_computation.43 | loop fusion | flops 8388608 | bytes 41951232 | tf_op jit(solution)/shard_map/mul | solution.py:65
  61.2 15.8 %maximum_reduce_fusion = f32[2,2,128,4096]{3,2,1,0:T(8,128)} fusion(f32[1,2,4,128,4096]{4,3,2,1,0:T(8,128)} %get-tuple-element.269, f32[1,2,4,128,4096]{4,3,2,1,0:T(8,128)} %get-tuple-element.268), kind=kLoop, calls=%fused_computation.33 | loop fusion | flops 14680064 | bytes 41943040 | tf_op jit(solution)/shard_map/reduce_sum | solution.py:131
  77.0 7.7 %slice_bitcast_fusion.1 = (f32[2,1,128,4096]{3,2,0,1:T(8,128)}, f32[2,1,128,4096]{3,2,0,1:T(8,128)}) fusion(f32[2,2,128,4096]{3,2,1,0:T(8,128)} %maximum_reduce_fusion), kind=kLoop, calls=%fused_computation.45 | loop fusion | bytes 16777216 | tf_op jit(solution)/shard_map/broadcast_in_dim;squeeze | solution.py:133
  84.7 7.2 copy.91
  97.5 7.2 copy.93
  104.7 86.4 %all-to-all-done = f32[2,1,128,4096]{2,0,1,3:T(2,128)} async-done(((f32[2,1,128,4096]{2,0,1,3:T(2,128)}), f32[2,1,128,4096]{2,0,1,3:T(2,128)}, u32[]{:S(2)}, u32[]{:S(2)}) %all-to-all-start) | async-done | bytes 4194336 | tf_op jit(solution)/shard_map/all_to_all | solution.py:133
  195.7 123.8 %while.18 = (s32[]{:T(128)}, f32[2,8,128,512]{3,2,1,0:T(8,128)}, f32[2,8,128,512]{3,2,1,0:T(8,128)}, f32[512,16]{0,1:T(8,128)}, f32[512,16]{0,1:T(8,128)}, /*ind...) while((s32[]{:T(128)}, f32[2,8,128,512]{3,2,1,0:T(8,128)}, ...), condition=%wide.region_2.3_spmd.clone.clone.clone, body=%wide.region_1.2_spmd.clone.clone.clone.sunk | while | flops 16823300 | bytes 16848104 | solution.py:29
  202.4 6.9 fusion.216
  210.3 6.9 fusion.216
  233.9 6.9 fusion.216
  241.8 6.9 fusion.216
  249.6 6.9 fusion.216
  257.5 6.9 fusion.216
  312.6 6.9 fusion.216
  341.4 7.1 fusion.36
  358.3 8.0 %fusion.28 = (f32[2,8,128,512]{3,1,2,0:T(8,128)}, f32[2,8,128,512]{3,1,2,0:T(8,128)}) fusion(f32[2,128,512,8]{2,3,1,0:T(8,128)S(1)} %convolution_subtract_fusion.3, f32[2,8,128]{1,2,0:T(8,128)S(1)} %copy.95, f32[2,8,128]{1,2,0:T(8,128)S(1)} %copy.90, f32[2,128,512,8]{2,3,1,0:T(8,128)S(1)} %fusion.32, f32[2,1,128,8,512]{4,3,2,0,1:T(8,128)S(1)} %copy-done.1, ...), kind=kOutput, calls=%fused_computation.54 | convolution fusion | flops 111149952 | bytes 25182336 | tf_op jit(solution)/shard_map/vi,qibc->qvbc/dot_general | solution.py:43
  371.8 7.0 fusion.50
  384.1 7.2 fusion.48
  413.9 6.9 subtract_bitcast_fusion.1
  426.3 8.5 %fusion.84 = f32[2,128,512,8]{2,3,1,0:T(8,128)} fusion(f32[2,8,128,512]{3,1,2,0:T(8,128)} %copy.105), kind=kOutput, calls=%fused_computation.137 | convolution fusion | flops 100664192 | bytes 8388608 | tf_op jit(solution)/shard_map/iv,qvbc->qibc/dot_general | solution.py:43
  475.2 85.7 %all-to-all-done.2 = f32[2,8,128,512]{3,2,0,1:T(8,128)} async-done(((f32[2,8,128,512]{3,2,0,1:T(8,128)}), f32[2,8,128,512]{3,2,0,1:T(8,128)}, u32[]{:S(2)}, u32[]{:S(2)}) %all-to-all-start.2) | async-done | bytes 4194336 | tf_op jit(solution)/shard_map/all_to_all | solution.py:138
  580.6 77.4 %all-to-all-done.3 = f32[2,8,128,512]{3,2,0,1:T(8,128)} async-done(((f32[2,8,128,512]{3,2,0,1:T(8,128)}), f32[2,8,128,512]{3,2,0,1:T(8,128)}, u32[]{:S(2)}, u32[]{:S(2)}) %all-to-all-start.3) | async-done | bytes 4194336 | tf_op jit(solution)/shard_map/all_to_all | solution.py:139
  680.5 70.0 %reduce-scatter.2.cloned.1.call-done = f32[128,4096]{1,0:T(8,128)} async-done(((f32[512,4096]{1,0:T(8,128)}), f32[128,4096]{1,0:T(8,128)}) %reduce-scatter.2.cloned.1.call-update) | async-done | bytes 2097168 | tf_op jit(solution)/shard_map/reduce_scatter | solution.py:143
  (140 shorter events, 245.9 us)
Async XLA Ops:
  6.5 39.6 %all-gather.2.cloned.1.call-start = ((), (), s32[]{:S(2)}) async-start(), calls=%async_computation.5 | async-start | bytes 5242880 | tf_op jit(solution)/shard_map/all_gather | solution.py:129
  91.9 99.2 %all-to-all-start = ((f32[2,1,128,4096]{2,0,1,3:T(2,128)}), f32[2,1,128,4096]{2,0,1,3:T(2,128)}, u32[]{:S(2)}, u32[]{:S(2)}) async-start(f32[2,1,128,4096]{2,0,1,3:T(2,128)} %copy.91), calls=%async_computation | async-start | bytes 8388608 | tf_op jit(solution)/shard_map/all_to_all | solution.py:133
  191.1 145.0 %all-to-all-start.1 = ((f32[2,1,128,4096]{2,0,1,3:T(2,128)}), f32[2,1,128,4096]{2,0,1,3:T(2,128)}, u32[]{:S(2)}, u32[]{:S(2)}) async-start(f32[2,1,128,4096]{2,0,1,3:T(2,128)} %copy.93), calls=%async_computation.1 | async-start | bytes 8388608 | tf_op jit(solution)/shard_map/all_to_all | solution.py:134
  341.4 7.1 copy-start
  341.4 7.1 copy-start.1
  384.1 7.2 copy-start.3
  384.1 7.2 copy-start.8
  391.2 3.7 copy-start.2
  391.3 3.7 copy-start.6
  391.3 4.6 copy-start.7
  440.2 6.0 copy-start.4
  440.2 6.0 copy-start.9
  446.2 5.2 copy-start.5
  462.4 98.4 %all-to-all-start.2 = ((f32[2,8,128,512]{3,2,0,1:T(8,128)}), f32[2,8,128,512]{3,2,0,1:T(8,128)}, u32[]{:S(2)}, u32[]{:S(2)}) async-start(f32[2,8,128,512]{3,2,0,1:T(8,128)} %copy.108), calls=%async_computation.2 | async-start | bytes 8388608 | tf_op jit(solution)/shard_map/all_to_all | solution.py:138
  560.8 97.1 %all-to-all-start.3 = ((f32[2,8,128,512]{3,2,0,1:T(8,128)}), f32[2,8,128,512]{3,2,0,1:T(8,128)}, u32[]{:S(2)}, u32[]{:S(2)}) async-start(f32[2,8,128,512]{3,2,0,1:T(8,128)} %copy.112), calls=%async_computation.3 | async-start | bytes 8388608 | tf_op jit(solution)/shard_map/all_to_all | solution.py:139
  565.4 185.1 %reduce-scatter.2.cloned.1.call-start = ((), (), s32[]{:S(2)}) async-start(), calls=%async_computation.6 | async-start | bytes 10485760 | tf_op jit(solution)/shard_map/reduce_scatter | solution.py:143
  680.5 70.0 %copy-start.10 = (bf16[128,4096]{1,0:T(8,128)(2,1)S(1)}, bf16[128,4096]{1,0:T(8,128)(2,1)}, u32[]{:S(2)}) copy-start(bf16[128,4096]{1,0:T(8,128)(2,1)} %param.7) | copy-start | bytes 3145732
  680.5 70.0 %copy-start.11 = (bf16[128,4096]{1,0:T(8,128)(2,1)S(1)}, bf16[128,4096]{1,0:T(8,128)(2,1)}, u32[]{:S(2)}) copy-start(bf16[128,4096]{1,0:T(8,128)(2,1)} %param.8) | copy-start | bytes 3145732
  680.5 70.0 %copy-start.12 = (f32[4096]{0:T(1024)S(1)}, f32[4096]{0:T(1024)}, u32[]{:S(2)}) copy-start(f32[4096]{0:T(1024)} %param.11) | copy-start | bytes 49156
Sparse Core Ops, SparseCore 0:
  8.9 37.1 all-gather.1
  680.6 69.8 reduce-scatter.1
where the time goes:
time: 770 us; the launch traced here: 761 us
  waiting for transfers between devices  359 us (47%)
  other arithmetic  165 us (21%)
  local copies, waits for them, and re-layouts  108 us (14%)
  matrix products  93.7 us (12%)
  starting transfers between devices  20.9 us (3%)
  between operations  14 us (2%)
    sub x16, other arithmetic, add_mode(): return (real_sum + quotient * den_real, imag_sum - quotient * den_imag)  108 us
    dot_general x16, matrix products, product(): return jnp.einsum(pattern, left, right, precision=lax.Precision.HIGHEST)  93.7 us
    all_to_all x1, waiting for transfers between devices, per_device(): lax.all_to_all(summed[0][:, None], 'inner', split_axis=3, concat_axis=1,...  86.4 us
    all_to_all x1, waiting for transfers between devices, per_device(): lax.all_to_all(real_w, 'inner', split_axis=1, concat_axis=3, tiled=True)  85.7 us
    all_to_all x1, waiting for transfers between devices, per_device(): lax.all_to_all(imag_w, 'inner', split_axis=1, concat_axis=3, tiled=True)  77.4 us
    reduce_scatter x1, waiting for transfers between devices, per_device(): lax.psum_scatter(inverse_terms(real_w, imag_w, tok_rows * lax.axis_size('...  70 us
    all_gather x1, waiting for transfers between devices, per_device(): lax.all_gather(signal, 'outer', axis=0, tiled=True)  38.7 us
    add x3, local copies, waits for them, and re-layouts, rotate(): sine * real_in + cosine * imag_in  17.4 us
  transfers between devices with their start and end apart: 6, of which 5 were waited for; matrix products, arithmetic and copies ran while one was open for 22% of the time, Pallas kernels for 0%

commit v1 on v0

v1 whole, which is shorter than its diff:
```python
import functools

import jax
import jax.numpy as jnp
from jax import lax
from jax.experimental import pallas as pl
from jax.experimental.pallas import tpu as pltpu
from jax.sharding import PartitionSpec as P

MESH = pl.DeviceIdType.MESH
LANES = 128
SUB = 8


def wrap(value, size):
    return lax.rem(value + size, size)


def tree_sum(terms):
    terms = list(terms)
    while len(terms) > 1:
        paired = [terms[i] + terms[i + 1] for i in range(0, len(terms) - 1, 2)]
        if len(terms) % 2:
            paired.append(terms[-1])
        terms = paired
    return terms[0]


def kernel(
    groups, inner, modes,
    par_ref, signal_ref, gating_ref, skip_ref, out_ref,
    par_buf, x_buf, y_buf, state_in, weight_in, state_out, state_got, carry_out,
    carry_got, total_buf, tap_buf,
    par_send, par_recv, state_send, state_recv, carry_send, carry_recv,
    total_send, total_recv,
):
    me = lax.axis_index("inner")
    block = lax.axis_index("outer")
    rows, channels = signal_ref.shape
    width = par_ref.shape[1]
    tiles = width // LANES
    steps = rows // SUB
    full = (SUB, LANES)
    seg = lax.broadcasted_iota(jnp.int32, full, 0)
    seg_f = seg.astype(jnp.float32)

    barrier = pltpu.get_barrier_semaphore()

    @pl.loop(1, inner)
    def _(r):
        pl.semaphore_signal(
            barrier, inc=1, device_id={"inner": wrap(me + r, inner)}, device_id_type=MESH
        )

    @pl.loop(1, groups)
    def _(r):
        pl.semaphore_signal(
            barrier, inc=1, device_id={"outer": wrap(block + r, groups)}, device_id_type=MESH
        )

    pl.semaphore_wait(barrier, inner + groups - 2)

    def par_copy(r):
        return pltpu.make_async_remote_copy(
            src_ref=par_ref, dst_ref=par_buf.at[r],
            send_sem=par_send.at[r], recv_sem=par_recv.at[r],
            device_id={"inner": wrap(me + r, inner)}, device_id_type=MESH,
        )

    def state_copy(r):
        return pltpu.make_async_remote_copy(
            src_ref=state_out.at[r], dst_ref=state_got.at[r],
            send_sem=state_send.at[r], recv_sem=state_recv.at[r],
            device_id={"inner": wrap(me - r, inner)}, device_id_type=MESH,
        )

    def carry_copy(r):
        return pltpu.make_async_remote_copy(
            src_ref=carry_out.at[r], dst_ref=carry_got.at[r],
            send_sem=carry_send.at[r], recv_sem=carry_recv.at[r],
            device_id={"inner": wrap(me + r, inner)}, device_id_type=MESH,
        )

    def total_copy(r):
        return pltpu.make_async_remote_copy(
            src_ref=total_buf.at[0], dst_ref=total_buf.at[r],
            send_sem=total_send.at[r], recv_sem=total_recv.at[r],
            device_id={"outer": wrap(block + r, groups)}, device_id_type=MESH,
        )

    @pl.loop(1, inner)
    def _(r):
        par_copy(r).start()

    par_buf[0] = par_ref[...]

    def place(r, tile):
        start = wrap(me - r, inner) * width + tile * LANES
        return (
            pl.ds(pl.multiple_of(start, LANES), LANES),
            pl.ds(pl.multiple_of(tile * LANES, LANES), LANES),
        )

    def rate_row(r, m, local):
        return jnp.broadcast_to(par_buf[r, m : m + 1, local], full)

    def weight_row(r, m, local):
        return jnp.broadcast_to(par_buf[r, modes + m : modes + m + 1, local], full)

    def end_states(r, tile):
        cols, local = place(r, tile)
        slot = r * tiles + tile
        x_buf[slot] = signal_ref[:, cols].astype(jnp.float32)
        rates = par_buf[r, 0:modes, local]
        for power, scale in enumerate((1.0, steps, 2.0 * steps, 4.0 * steps)):
            tap_buf[power * modes : (power + 1) * modes, :] = jnp.exp(rates * (-scale))

        def row(power, m):
            at = power * modes + m
            return jnp.broadcast_to(tap_buf[at : at + 1, :], full)

        decays = [row(0, m) for m in range(modes)]
        first = x_buf[slot, pl.ds(0, SUB, stride=steps), :]
        states = [first] * modes
        for j in range(1, steps):
            value = x_buf[slot, pl.ds(j, SUB, stride=steps), :]
            states = [decays[m] * states[m] + value for m in range(modes)]
        for m in range(modes):
            ends = states[m]
            for power, hop in ((1, 1), (2, 2), (3, 4)):
                moved = jnp.where(seg >= hop, pltpu.roll(ends, hop, 0), 0.0)
                ends = ends + row(power, m) * moved
            state_in[slot, m] = ends
            state_out[r, m : m + 1, local] = ends[SUB - 1 : SUB, :]

    def within(r, tile):
        cols, local = place(r, tile)
        slot = r * tiles + tile
        taps = [jnp.zeros(full, jnp.float32) for _ in range(steps // SUB)]
        for m in range(modes):
            rate = rate_row(r, m, local)
            weight = weight_row(r, m, local)
            for part in range(steps // SUB):
                taps[part] = taps[part] + weight * jnp.exp(-rate * (seg_f + float(part * SUB)))
            ends = jnp.where(seg >= 1, pltpu.roll(state_in[slot, m], 1, 0), 0.0)
            state_in[slot, m] = ends * (weight * jnp.exp(-rate))
            weight_in[slot, m] = weight * jnp.exp(-rate * (seg_f * float(steps) + 1.0))
        for part in range(steps // SUB):
            tap_buf[part * SUB : (part + 1) * SUB, :] = taps[part]
        values = [x_buf[slot, pl.ds(j, SUB, stride=steps), :] for j in range(steps)]
        filters = [jnp.broadcast_to(tap_buf[j : j + 1, :], full) for j in range(steps)]
        for j in range(steps):
            y_buf[slot, pl.ds(j, SUB, stride=steps), :] = tree_sum(
                [filters[k] * values[j - k] for k in range(j + 1)]
            )

    def finish(r, tile):
        cols, local = place(r, tile)
        slot = r * tiles + tile
        terms = []
        decays = []
        for m in range(modes):
            carry = jnp.broadcast_to(carry_got[r, m : m + 1, local], full)
            terms.append(state_in[slot, m] + weight_in[slot, m] * carry)
        tap_buf[0:modes, :] = jnp.exp(-par_buf[r, 0:modes, local])
        decays = [jnp.broadcast_to(tap_buf[m : m + 1, :], full) for m in range(modes)]
        for j in range(steps):
            at = pl.ds(j, SUB, stride=steps)
            y_buf[slot, at, :] = y_buf[slot, at, :] + tree_sum(terms)
            if j + 1 < steps:
                terms = [terms[m] * decays[m] for m in range(modes)]
        skip = jnp.broadcast_to(skip_ref[:, cols], (2 * SUB, LANES))
        for part in range(rows // (2 * SUB)):
            at = slice(part * 2 * SUB, (part + 1) * 2 * SUB)
            gate = gating_ref[at, cols].astype(jnp.float32)
            out_ref[at, cols] = (
                gate * (y_buf[slot, at, :] + skip * x_buf[slot, at, :])
            ).astype(jnp.bfloat16)

    def sweep(low, high, body):
        @pl.loop(low * tiles, high * tiles)
        def _(i):
            body(i // tiles, i % tiles)

    @pl.loop(0, inner)
    def _(r):
        @pl.when(r > 0)
        def _():
            par_copy(r).wait_recv()

        @pl.loop(0, tiles)
        def _(tile):
            end_states(r, tile)

        @pl.when(r > 0)
        def _():
            state_copy(r).start()

    cut_a = inner // 2
    cut_b = (3 * inner) // 4
    sweep(0, cut_a, within)

    @pl.loop(1, inner)
    def _(r):
        state_copy(r).wait_recv()

    state_got[0] = state_out[0]
    rates = par_buf[0, 0:modes, :]
    decay_block = jnp.exp(rates * (-float(rows)))

    def advance(b, run):
        at = wrap(b - me, inner)
        carry_out[at] = run
        return decay_block * run + state_got[at]

    total = lax.fori_loop(0, inner, advance, jnp.zeros((modes, width), jnp.float32))
    total_buf[0] = total

    @pl.loop(1, groups)
    def _(r):
        total_copy(r).start()

    sweep(cut_a, cut_b, within)

    @pl.loop(1, groups)
    def _(r):
        total_copy(r).wait_recv()

    decay_group = jnp.exp(rates * (-float(rows * inner)))

    def join(b, run):
        got = total_buf[wrap(block - b, groups)]
        return jnp.where(b < block, decay_group * run + got, run)

    before = lax.fori_loop(0, groups, join, jnp.zeros((modes, width), jnp.float32))

    @pl.loop(0, inner)
    def _(r):
        b = wrap(me + r, inner)
        reach = (b * (-rows)).astype(jnp.float32)
        carry_out[r] = carry_out[r] + jnp.exp(rates * reach) * before

        @pl.when(r > 0)
        def _():
            carry_copy(r).start()

    carry_got[0] = carry_out[0]
    sweep(cut_b, inner, within)

    @pl.loop(0, inner)
    def _(r):
        @pl.when(r > 0)
        def _():
            carry_copy(r).wait_recv()

        @pl.loop(0, tiles)
        def _(tile):
            finish(r, tile)

    @pl.loop(1, inner)
    def _(r):
        par_copy(r).wait_send()
        state_copy(r).wait_send()
        carry_copy(r).wait_send()

    @pl.loop(1, groups)
    def _(r):
        total_copy(r).wait_send()


def per_device(signal, gating, decay_rate, residues, skip_gain):
    groups = lax.axis_size("outer")
    inner = lax.axis_size("inner")
    rows, channels = signal.shape
    width, modes = decay_rate.shape
    tiles = width // LANES
    weights = residues * jnp.sqrt(-jnp.expm1(-2.0 * decay_rate))
    params = jnp.concatenate([decay_rate.T, weights.T], axis=0)
    f32 = jnp.float32
    dma = pltpu.SemaphoreType.DMA
    part = (inner, modes, width)
    return pl.pallas_call(
        functools.partial(kernel, groups, inner, modes),
        out_shape=jax.ShapeDtypeStruct((rows, channels), jnp.bfloat16),
        in_specs=[pl.BlockSpec(memory_space=pltpu.VMEM)] * 4,
        out_specs=pl.BlockSpec(memory_space=pltpu.VMEM),
        scratch_shapes=[
            pltpu.VMEM((inner, 2 * modes, width), f32),
            pltpu.VMEM((inner * tiles, rows, LANES), f32),
            pltpu.VMEM((inner * tiles, rows, LANES), f32),
            pltpu.VMEM((inner * tiles, modes, SUB, LANES), f32),
            pltpu.VMEM((inner * tiles, modes, SUB, LANES), f32),
            pltpu.VMEM(part, f32),
            pltpu.VMEM(part, f32),
            pltpu.VMEM(part, f32),
            pltpu.VMEM(part, f32),
            pltpu.VMEM((groups, modes, width), f32),
            pltpu.VMEM((4 * modes, LANES), f32),
            dma((inner,)), dma((inner,)), dma((inner,)), dma((inner,)),
            dma((inner,)), dma((inner,)), dma((groups,)), dma((groups,)),
        ],
        compiler_params=pltpu.CompilerParams(
            collective_id=0, has_side_effects=True, vmem_limit_bytes=40 * 1024 * 1024
        ),
        name="modal_scan",
    )(params, signal, gating, skip_gain[None, :])


def solution(mesh):
    return jax.shard_map(
        per_device,
        mesh=mesh,
        in_specs=(
            P(("outer", "inner"), None),
            P(("outer", "inner"), None),
            P("inner", None),
            P("inner", None),
            P(),
        ),
        out_specs=P(("outer", "inner"), None),
        check_vma=False,
    )
```

time: 770 us -> 43.6 us (0.06); the launches traced: 761 us -> 43.3 us
  waiting for transfers between devices: 359 us -> 0 us
  other arithmetic: 165 us -> 0.87 us
  local copies, waits for them, and re-layouts: 108 us -> 4.12 us
  matrix products: 93.7 us -> 0 us
  Pallas kernels: 0 us -> 38.3 us
  starting transfers between devices: 20.9 us -> 0 us
  between operations: 14 us -> 0.04 us
    all_to_all x4 -> x0, waiting for transfers between devices: 249 us -> none  [the longest x1 86.4 us: per_device(): lax.all_to_all(summed[0][:, None], 'inner', split_axis=3, concat_axis=1,...]
    sub x16 -> x0, other arithmetic: 108 us -> none  [add_mode(): return (real_sum + quotient * den_real, imag_sum - quotient * den_imag)]
    dot_general x16 -> x0, matrix products: 93.7 us -> none  [product(): return jnp.einsum(pattern, left, right, precision=lax.Precision.HIGHEST)]
    reduce_scatter x1 -> x0, waiting for transfers between devices: 70 us -> none  [per_device(): lax.psum_scatter(inverse_terms(real_w, imag_w, tok_rows * lax.axis_size('...]
    all_gather x1 -> x0, waiting for transfers between devices: 38.7 us -> none  [per_device(): lax.all_gather(signal, 'outer', axis=0, tiled=True)]
    pallas_call x0 -> x1, Pallas kernels: none -> 38.3 us  [per_device(): pl.pallas_call(functools.partial(kernel, groups, inner, modes), out_shape...]
    mul x53 -> x0, other arithmetic: 37.6 us -> none  [the longest x2 15.1 us: outer_terms(): return jnp.stack([jnp.cos(angles) * values_f, jnp.sin(angles) * values_f])]
    add x5 -> x0, local copies, waits for them, and re-layouts: 22.3 us -> none  [the longest x3 17.4 us: rotate(): sine * real_in + cosine * imag_in]
  transfers between devices with their start and end apart: 6 -> 0, of which waited for: 5 -> 0; matrix products, arithmetic and copies ran while one was open for 22% -> 0% of each run, Pallas kernels for 0% -> 0%
where the time goes in v1:
time: 43.6 us; the launch traced here: 43.3 us
  Pallas kernels  38.3 us (88%)
  local copies, waits for them, and re-layouts  4.12 us (9%)
  other arithmetic  0.87 us (2%)
    pallas_call x1, Pallas kernels, per_device(): pl.pallas_call(functools.partial(kernel, groups, inner, modes), out_shape...  38.3 us
    unnamed x9, local copies, waits for them, and re-layouts  4.12 us

profile of v1, /device:TPU:0, one launch (start us, length us, event | category | flops | bytes accessed | tf_op | source)
XLA Modules:
  0.0 43.3 jit_solution(6279976296212682836)
XLA Ops:
  0.0 0.0 copy-start.3
  0.0 0.9 %multiply_bitcast_fusion = f32[16,512]{1,0:T(8,128)S(1)} fusion(f32[512,16]{0,1:T(8,128)} %param.8, f32[512,16]{0,1:T(8,128)} %param.7), kind=kLoop, calls=%fused_computation.1 | loop fusion | flops 24576 | bytes 98304 | tf_op jit(solution)/shard_map/transpose | solution.py:278
  0.9 0.0 copy-done.3
  0.9 0.0 copy-start.2
  0.9 0.7 %copy-done.2 = f32[4096]{0:T(1024)S(1)} copy-done((f32[4096]{0:T(1024)S(1)}, f32[4096]{0:T(1024)}, u32[]{:S(2)}) %copy-start.2) | copy-done | bytes 16408
  1.6 0.0 copy-start
  1.6 1.2 %copy-done = bf16[128,4096]{1,0:T(8,128)(2,1)S(1)} copy-done((bf16[128,4096]{1,0:T(8,128)(2,1)S(1)}, bf16[128,4096]{1,0:T(8,128)(2,1)}, u32[]{:S(2)}) %copy-start) | copy-done | bytes 1048600
  2.8 0.0 copy-start.1
  2.8 1.2 %copy-done.1 = bf16[128,4096]{1,0:T(8,128)(2,1)S(1)} copy-done((bf16[128,4096]{1,0:T(8,128)(2,1)S(1)}, bf16[128,4096]{1,0:T(8,128)(2,1)}, u32[]{:S(2)}) %copy-start.1) | copy-done | bytes 1048600
  4.0 38.3 %modal_scan.1 = bf16[128,4096]{1,0:T(8,128)(2,1)S(1)} custom-call(f32[32,512]{1,0:T(8,128)S(1)} %pad_maximum_fusion.par_ref, bf16[128,4096]{1,0:T(8,128)(2,1)S(1)} %copy-done, bf16[128,4096]{1,0:T(8,128)(2,1)S(1)} %copy-done.1, f32[1,4096]{1,0:T(1,128)S(1)} %bitcast.4), custom_call_target="tpu_custom_call" | custom-call | tf_op jit(solution)/shard_map/modal_scan/pallas_call | solution.py:282
  42.3 1.0 %copy.7 = bf16[128,4096]{1,0:T(8,128)(2,1)} copy(bf16[128,4096]{1,0:T(8,128)(2,1)S(1)} %modal_scan.1) | data formatting | bytes 2097152
  (1 shorter events, 0.0 us)
Async XLA Ops:
  0.0 0.9 %copy-start.3 = (f32[512,16]{0,1:T(8,128)S(1)}, f32[512,16]{0,1:T(8,128)}, u32[]{:S(2)}) copy-start(f32[512,16]{0,1:T(8,128)} %param.7) | copy-start | bytes 98308
  0.9 0.7 %copy-start.2 = (f32[4096]{0:T(1024)S(1)}, f32[4096]{0:T(1024)}, u32[]{:S(2)}) copy-start(f32[4096]{0:T(1024)} %param.9) | copy-start | bytes 49156
  1.6 1.2 %copy-start = (bf16[128,4096]{1,0:T(8,128)(2,1)S(1)}, bf16[128,4096]{1,0:T(8,128)(2,1)}, u32[]{:S(2)}) copy-start(bf16[128,4096]{1,0:T(8,128)(2,1)} %signal_ref.1) | copy-start | bytes 3145732
  2.8 1.2 %copy-start.1 = (bf16[128,4096]{1,0:T(8,128)(2,1)S(1)}, bf16[128,4096]{1,0:T(8,128)(2,1)}, u32[]{:S(2)}) copy-start(bf16[128,4096]{1,0:T(8,128)(2,1)} %gating_ref.1) | copy-start | bytes 3145732

commit v2 on v1

--- a/solution.py
+++ b/solution.py
@@ -26,18 +26,28 @@
     return terms[0]
 
 
+def one_minus_exp(z):
+    series = jnp.ones_like(z)
+    for n in range(12, 1, -1):
+        series = 1.0 - series * z * (1.0 / n)
+    return jnp.where(z < 0.5, z * series, 1.0 - jnp.exp(-z))
+
+
 def kernel(
     groups, inner, modes,
-    par_ref, signal_ref, gating_ref, skip_ref, out_ref,
+    rate_hbm, residue_hbm, signal_hbm, gating_hbm, skip_hbm, out_ref,
+    rate_ref, residue_ref, signal_ref, gating_ref, skip_ref,
     par_buf, x_buf, y_buf, state_in, weight_in, state_out, state_got, carry_out,
     carry_got, total_buf, tap_buf,
-    par_send, par_recv, state_send, state_recv, carry_send, carry_recv,
-    total_send, total_recv,
+    load_sem, par_send, par_recv, core_send, core_recv, state_send, state_recv,
+    carry_send, carry_recv, total_send, total_recv,
 ):
     me = lax.axis_index("inner")
     block = lax.axis_index("outer")
+    half = lax.rem(block, 2)
+    twin = block + 1 - 2 * half
     rows, channels = signal_ref.shape
-    width = par_ref.shape[1]
+    width = rate_ref.shape[1]
     tiles = width // LANES
     steps = rows // SUB
     full = (SUB, LANES)
@@ -58,60 +68,80 @@
             barrier, inc=1, device_id={"outer": wrap(block + r, groups)}, device_id_type=MESH
         )
 
+    loads = [
+        pltpu.make_async_copy(source, target, load_sem.at[n])
+        for n, (source, target) in enumerate((
+            (rate_hbm, rate_ref), (residue_hbm, residue_ref), (signal_hbm, signal_ref),
+            (gating_hbm, gating_ref), (skip_hbm, skip_ref),
+        ))
+    ]
+    for load in loads:
+        load.start()
+
+    def remote(source, target, send, recv, device):
+        return pltpu.make_async_remote_copy(
+            src_ref=source, dst_ref=target, send_sem=send, recv_sem=recv,
+            device_id=device, device_id_type=MESH,
+        )
+
+    def par_copy(r):
+        return remote(
+            par_buf.at[0, half], par_buf.at[r, half],
+            par_send.at[r], par_recv.at[r], {"inner": wrap(me + r, inner)},
+        )
+
+    def par_core(r):
+        return remote(
+            par_buf.at[r, half], par_buf.at[r, half],
+            core_send.at[r], core_recv.at[r], {"outer": twin},
+        )
+
+    def state_copy(r):
+        return remote(
+            state_out.at[r], state_got.at[r],
+            state_send.at[r], state_recv.at[r], {"inner": wrap(me - r, inner)},
+        )
+
+    def carry_copy(r):
+        return remote(
+            carry_out.at[r], carry_got.at[r],
+            carry_send.at[r], carry_recv.at[r], {"inner": wrap(me + r, inner)},
+        )
+
+    def total_copy(r):
+        return remote(
+            total_buf.at[0], total_buf.at[r],
+            total_send.at[r], total_recv.at[r], {"outer": wrap(block + r, groups)},
+        )
+
+    loads[0].wait()
+    loads[1].wait()
+    par_buf[0, 0] = rate_ref[...]
+    par_buf[0, 1] = residue_ref[...] * jnp.sqrt(one_minus_exp(2.0 * rate_ref[...]))
     pl.semaphore_wait(barrier, inner + groups - 2)
 
-    def par_copy(r):
-        return pltpu.make_async_remote_copy(
-            src_ref=par_ref, dst_ref=par_buf.at[r],
-            send_sem=par_send.at[r], recv_sem=par_recv.at[r],
-            device_id={"inner": wrap(me + r, inner)}, device_id_type=MESH,
-        )
-
-    def state_copy(r):
-        return pltpu.make_async_remote_copy(
-            src_ref=state_out.at[r], dst_ref=state_got.at[r],
-            send_sem=state_send.at[r], recv_sem=state_recv.at[r],
-            device_id={"inner": wrap(me - r, inner)}, device_id_type=MESH,
-        )
-
-    def carry_copy(r):
-        return pltpu.make_async_remote_copy(
-            src_ref=carry_out.at[r], dst_ref=carry_got.at[r],
-            send_sem=carry_send.at[r], recv_sem=carry_recv.at[r],
-            device_id={"inner": wrap(me + r, inner)}, device_id_type=MESH,
-        )
-
-    def total_copy(r):
-        return pltpu.make_async_remote_copy(
-            src_ref=total_buf.at[0], dst_ref=total_buf.at[r],
-            send_sem=total_send.at[r], recv_sem=total_recv.at[r],
-            device_id={"outer": wrap(block + r, groups)}, device_id_type=MESH,
-        )
-
     @pl.loop(1, inner)
     def _(r):
         par_copy(r).start()
 
-    par_buf[0] = par_ref[...]
-
-    def place(r, tile):
-        start = wrap(me - r, inner) * width + tile * LANES
+    def place(slot, tile):
+        start = wrap(me - slot, inner) * width + tile * LANES
         return (
             pl.ds(pl.multiple_of(start, LANES), LANES),
             pl.ds(pl.multiple_of(tile * LANES, LANES), LANES),
         )
 
     def rate_row(r, m, local):
-        return jnp.broadcast_to(par_buf[r, m : m + 1, local], full)
+        return jnp.broadcast_to(par_buf[r, 0, m : m + 1, local], full)
 
     def weight_row(r, m, local):
-        return jnp.broadcast_to(par_buf[r, modes + m : modes + m + 1, local], full)
+        return jnp.broadcast_to(par_buf[r, 1, m : m + 1, local], full)
 
     def end_states(r, tile):
         cols, local = place(r, tile)
         slot = r * tiles + tile
         x_buf[slot] = signal_ref[:, cols].astype(jnp.float32)
-        rates = par_buf[r, 0:modes, local]
+        rates = par_buf[r, 0, :, local]
         for power, scale in enumerate((1.0, steps, 2.0 * steps, 4.0 * steps)):
             tap_buf[power * modes : (power + 1) * modes, :] = jnp.exp(rates * (-scale))
 
@@ -162,7 +192,7 @@
         for m in range(modes):
             carry = jnp.broadcast_to(carry_got[r, m : m + 1, local], full)
             terms.append(state_in[slot, m] + weight_in[slot, m] * carry)
-        tap_buf[0:modes, :] = jnp.exp(-par_buf[r, 0:modes, local])
+        tap_buf[0:modes, :] = jnp.exp(-par_buf[r, 0, :, local])
         decays = [jnp.broadcast_to(tap_buf[m : m + 1, :], full) for m in range(modes)]
         for j in range(steps):
             at = pl.ds(j, SUB, stride=steps)
@@ -182,19 +212,26 @@
         def _(i):
             body(i // tiles, i % tiles)
 
-    @pl.loop(0, inner)
-    def _(r):
-        @pl.when(r > 0)
-        def _():
-            par_copy(r).wait_recv()
-
+    def end_slot(slot):
         @pl.loop(0, tiles)
         def _(tile):
-            end_states(r, tile)
-
-        @pl.when(r > 0)
+            end_states(slot, tile)
+
+    loads[2].wait()
+    end_slot(0)
+    par_copy(1).wait_recv()
+    par_core(1).start()
+
+    @pl.loop(1, inner)
+    def _(r):
+        @pl.when(r + 1 < inner)
         def _():
-            state_copy(r).start()
+            par_copy(r + 1).wait_recv()
+            par_core(r + 1).start()
+
+        par_core(r).wait_recv()
+        end_slot(r)
+        state_copy(r).start()
 
     cut_a = inner // 2
     cut_b = (3 * inner) // 4
@@ -205,7 +242,7 @@
         state_copy(r).wait_recv()
 
     state_got[0] = state_out[0]
-    rates = par_buf[0, 0:modes, :]
+    rates = par_buf[0, 0]
     decay_block = jnp.exp(rates * (-float(rows)))
 
     def advance(b, run):
@@ -246,6 +283,8 @@
 
     carry_got[0] = carry_out[0]
     sweep(cut_b, inner, within)
+    loads[3].wait()
+    loads[4].wait()
 
     @pl.loop(0, inner)
     def _(r):
@@ -260,6 +299,7 @@
     @pl.loop(1, inner)
     def _(r):
         par_copy(r).wait_send()
+        par_core(r).wait_send()
         state_copy(r).wait_send()
         carry_copy(r).wait_send()
 
@@ -274,36 +314,38 @@
     rows, channels = signal.shape
     width, modes = decay_rate.shape
     tiles = width // LANES
-    weights = residues * jnp.sqrt(-jnp.expm1(-2.0 * decay_rate))
-    params = jnp.concatenate([decay_rate.T, weights.T], axis=0)
     f32 = jnp.float32
     dma = pltpu.SemaphoreType.DMA
-    part = (inner, modes, width)
+
+    def states(count):
+        return pltpu.VMEM((count, modes, width), f32)
+
     return pl.pallas_call(
         functools.partial(kernel, groups, inner, modes),
         out_shape=jax.ShapeDtypeStruct((rows, channels), jnp.bfloat16),
-        in_specs=[pl.BlockSpec(memory_space=pltpu.VMEM)] * 4,
+        in_specs=[pl.BlockSpec(memory_space=pltpu.HBM)] * 5,
         out_specs=pl.BlockSpec(memory_space=pltpu.VMEM),
         scratch_shapes=[
-            pltpu.VMEM((inner, 2 * modes, width), f32),
+            pltpu.VMEM((modes, width), f32),
+            pltpu.VMEM((modes, width), f32),
+            pltpu.VMEM((rows, channels), jnp.bfloat16),
+            pltpu.VMEM((rows, channels), jnp.bfloat16),
+            pltpu.VMEM((1, channels), f32),
+            pltpu.VMEM((inner, 2, modes, width), f32),
             pltpu.VMEM((inner * tiles, rows, LANES), f32),
             pltpu.VMEM((inner * tiles, rows, LANES), f32),
             pltpu.VMEM((inner * tiles, modes, SUB, LANES), f32),
             pltpu.VMEM((inner * tiles, modes, SUB, LANES), f32),
-            pltpu.VMEM(part, f32),
-            pltpu.VMEM(part, f32),
-            pltpu.VMEM(part, f32),
-            pltpu.VMEM(part, f32),
-            pltpu.VMEM((groups, modes, width), f32),
+            states(inner), states(inner), states(inner), states(inner), states(groups),
             pltpu.VMEM((4 * modes, LANES), f32),
-            dma((inner,)), dma((inner,)), dma((inner,)), dma((inner,)),
-            dma((inner,)), dma((inner,)), dma((groups,)), dma((groups,)),
+            dma((5,)), dma((inner,)), dma((inner,)), dma((inner,)), dma((inner,)), dma((inner,)),
+            dma((inner,)), dma((inner,)), dma((inner,)), dma((groups,)), dma((groups,)),
         ],
         compiler_params=pltpu.CompilerParams(
-            collective_id=0, has_side_effects=True, vmem_limit_bytes=40 * 1024 * 1024
+            collective_id=0, has_side_effects=True, vmem_limit_bytes=63 * 1024 * 1024
         ),
         name="modal_scan",
-    )(params, signal, gating, skip_gain[None, :])
+    )(decay_rate.T, residues.T, signal, gating, skip_gain[None, :])
 
 
 def solution(mesh):

time: 43.6 us -> 35.6 us (0.82)
  Pallas kernels: 38.3 us -> 33.1 us
  local copies, waits for them, and re-layouts: 4.12 us -> 2.29 us
  other arithmetic: 0.87 us -> 0 us
    pallas_call x1, Pallas kernels: 38.3 us -> 33.1 us  [per_device(): pl.pallas_call(functools.partial(kernel, groups, inner, modes), out_shape...]
    unnamed x9 -> x1, local copies, waits for them, and re-layouts: 4.12 us -> 2.29 us
    transpose x1 -> x0, other arithmetic: 0.86 us -> none  [per_device(): params = jnp.concatenate([decay_rate.T, weights.T], axis=0)]
where the time goes in v2:
time: 35.6 us; the launch traced here: 35.4 us
  Pallas kernels  33.1 us (93%)
  local copies, waits for them, and re-layouts  2.29 us (6%)
    pallas_call x1, Pallas kernels, per_device(): pl.pallas_call(functools.partial(kernel, groups, inner, modes), out_shape...  33.1 us
    unnamed x1, local copies, waits for them, and re-layouts  2.29 us

profile of v2, /device:TPU:0, one launch (start us, length us, event | category | flops | bytes accessed | tf_op | source)
XLA Modules:
  0.0 35.4 jit_solution(3612676312907129359)
XLA Ops:
  0.0 33.1 %modal_scan.1 = bf16[128,4096]{1,0:T(8,128)(2,1)} custom-call(f32[16,512]{1,0:T(8,128)} %bitcast.3, f32[16,512]{1,0:T(8,128)} %bitcast.4, bf16[128,4096]{1,0:T(8,128)(2,1)} %signal_hbm.1, bf16[128,4096]{1,0:T(8,128)(2,1)} %gating_hbm.1, f32[1,4096]{1,0:T(1,128)} %bitcast.5), custom_call_target="tpu_custom_call" | custom-call | tf_op jit(solution)/shard_map/modal_scan/pallas_call | solution.py:323
  33.2 2.3 %copy.7 = bf16[128,4096]{1,0:T(8,128)(2,1)} copy(bf16[128,4096]{1,0:T(8,128)(2,1)} %modal_scan.1) | data formatting | bytes 2097152

commit v3 on v2

v3 whole, which is shorter than its diff:
```python
import functools

import jax
import jax.numpy as jnp
from jax import lax
from jax.experimental import pallas as pl
from jax.experimental.pallas import tpu as pltpu
from jax.sharding import PartitionSpec as P

MESH = pl.DeviceIdType.MESH
LANES = 128
SUB = 8
CHUNKS = 1


def wrap(value, size):
    return lax.rem(value + size, size)


def tree_sum(terms):
    terms = list(terms)
    while len(terms) > 1:
        paired = [terms[i] + terms[i + 1] for i in range(0, len(terms) - 1, 2)]
        if len(terms) % 2:
            paired.append(terms[-1])
        terms = paired
    return terms[0]


def one_minus_exp(z):
    series = jnp.ones_like(z)
    for n in range(12, 1, -1):
        series = 1.0 - series * z * (1.0 / n)
    return jnp.where(z < 0.5, z * series, 1.0 - jnp.exp(-z))


def kernel(
    groups, inner, modes,
    rate_hbm, residue_hbm, signal_hbm, gating_hbm, skip_hbm, out_hbm,
    rate_ref, residue_ref, signal_ref, gating_ref, skip_ref,
    out_buf, par_buf, x_buf, y_buf, state_in, weight_in, state_out, state_got, carry_out,
    carry_got, total_buf, tap_buf,
    load_sem, out_sem, par_send, par_recv, core_send, core_recv, state_send, state_recv,
    carry_send, carry_recv, total_send, total_recv,
):
    me = lax.axis_index("inner")
    block = lax.axis_index("outer")
    half = lax.rem(block, 2)
    twin = block + 1 - 2 * half
    rows, channels = signal_ref.shape
    width = rate_ref.shape[1]
    tiles = width // LANES
    steps = rows // SUB
    part = modes // CHUNKS
    full = (SUB, LANES)
    seg = lax.broadcasted_iota(jnp.int32, full, 0)
    seg_f = seg.astype(jnp.float32)

    barrier = pltpu.get_barrier_semaphore()

    @pl.loop(1, inner)
    def _(r):
        pl.semaphore_signal(
            barrier, inc=1, device_id={"inner": wrap(me + r, inner)}, device_id_type=MESH
        )

    @pl.loop(1, groups)
    def _(r):
        pl.semaphore_signal(
            barrier, inc=1, device_id={"outer": wrap(block + r, groups)}, device_id_type=MESH
        )

    loads = [
        pltpu.make_async_copy(source, target, load_sem.at[n])
        for n, (source, target) in enumerate((
            (rate_hbm, rate_ref), (residue_hbm, residue_ref), (signal_hbm, signal_ref),
            (gating_hbm, gating_ref), (skip_hbm, skip_ref),
        ))
    ]
    for load in loads:
        load.start()

    def remote(source, target, send, recv, device):
        return pltpu.make_async_remote_copy(
            src_ref=source, dst_ref=target, send_sem=send, recv_sem=recv,
            device_id=device, device_id_type=MESH,
        )

    def par_copy(c, r):
        return remote(
            par_buf.at[c, 0, half], par_buf.at[c, r, half],
            par_send.at[c, r], par_recv.at[c, r], {"inner": wrap(me + r, inner)},
        )

    def par_core(c, r):
        return remote(
            par_buf.at[c, r, half], par_buf.at[c, r, half],
            core_send.at[c, r], core_recv.at[c, r], {"outer": twin},
        )

    def state_copy(c, r):
        return remote(
            state_out.at[c, r], state_got.at[c, r],
            state_send.at[c, r], state_recv.at[c, r], {"inner": wrap(me - r, inner)},
        )

    def carry_copy(c, r):
        return remote(
            carry_out.at[c, r], carry_got.at[c, r],
            carry_send.at[c, r], carry_recv.at[c, r], {"inner": wrap(me + r, inner)},
        )

    def total_copy(c, r):
        return remote(
            total_buf.at[c, 0], total_buf.at[c, r],
            total_send.at[c, r], total_recv.at[c, r], {"outer": wrap(block + r, groups)},
        )

    def out_copy(slot):
        start = wrap(me - slot, inner) * width
        cols = pl.ds(pl.multiple_of(start, LANES), width)
        return pltpu.make_async_copy(
            out_buf.at[:, cols], out_hbm.at[:, cols], out_sem.at[slot]
        )

    loads[0].wait()
    loads[1].wait()
    for c in range(CHUNKS):
        at = slice(c * part, (c + 1) * part)
        par_buf[c, 0, 0] = rate_ref[at]
        par_buf[c, 0, 1] = residue_ref[at] * jnp.sqrt(one_minus_exp(2.0 * rate_ref[at]))
    pl.semaphore_wait(barrier, inner + groups - 2)

    for c in range(CHUNKS):
        @pl.loop(1, inner)
        def _(r):
            par_copy(c, r).start()

    def place(slot, tile):
        start = wrap(me - slot, inner) * width + tile * LANES
        return (
            pl.ds(pl.multiple_of(start, LANES), LANES),
            pl.ds(pl.multiple_of(tile * LANES, LANES), LANES),
        )

    def rate_row(r, m, local):
        at = m % part
        return jnp.broadcast_to(par_buf[m // part, r, 0, at : at + 1, local], full)

    def weight_row(r, m, local):
        at = m % part
        return jnp.broadcast_to(par_buf[m // part, r, 1, at : at + 1, local], full)

    def end_states(c, r, tile):
        cols, local = place(r, tile)
        slot = r * tiles + tile
        rates = par_buf[c, r, 0, :, local]
        for power, scale in enumerate((1.0, steps, 2.0 * steps, 4.0 * steps)):
            tap_buf[power * part : (power + 1) * part, :] = jnp.exp(rates * (-scale))

        def row(power, m):
            at = power * part + m
            return jnp.broadcast_to(tap_buf[at : at + 1, :], full)

        decays = [row(0, m) for m in range(part)]
        first = x_buf[slot, pl.ds(0, SUB, stride=steps), :]
        states = [first] * part
        for j in range(1, steps):
            value = x_buf[slot, pl.ds(j, SUB, stride=steps), :]
            states = [decays[m] * states[m] + value for m in range(part)]
        for m in range(part):
            ends = states[m]
            for power, hop in ((1, 1), (2, 2), (3, 4)):
                moved = jnp.where(seg >= hop, pltpu.roll(ends, hop, 0), 0.0)
                ends = ends + row(power, m) * moved
            state_in[slot, c * part + m] = ends
            state_out[c, r, m : m + 1, local] = ends[SUB - 1 : SUB, :]

    def within(r, tile):
        cols, local = place(r, tile)
        slot = r * tiles + tile
        taps = [jnp.zeros(full, jnp.float32) for _ in range(steps // SUB)]
        for m in range(modes):
            rate = rate_row(r, m, local)
            weight = weight_row(r, m, local)
            for n in range(steps // SUB):
                taps[n] = taps[n] + weight * jnp.exp(-rate * (seg_f + float(n * SUB)))
            ends = jnp.where(seg >= 1, pltpu.roll(state_in[slot, m], 1, 0), 0.0)
            state_in[slot, m] = ends * (weight * jnp.exp(-rate))
            weight_in[slot, m] = weight * jnp.exp(-rate * (seg_f * float(steps) + 1.0))
        for n in range(steps // SUB):
            tap_buf[n * SUB : (n + 1) * SUB, :] = taps[n]
        values = [x_buf[slot, pl.ds(j, SUB, stride=steps), :] for j in range(steps)]
        filters = [jnp.broadcast_to(tap_buf[j : j + 1, :], full) for j in range(steps)]
        for j in range(steps):
            y_buf[slot, pl.ds(j, SUB, stride=steps), :] = tree_sum(
                [filters[k] * values[j - k] for k in range(j + 1)]
            )

    def finish(r, tile):
        cols, local = place(r, tile)
        slot = r * tiles + tile
        terms = []
        decays = []
        for m in range(modes):
            at = m % part
            carry = jnp.broadcast_to(carry_got[m // part, r, at : at + 1, local], full)
            terms.append(state_in[slot, m] + weight_in[slot, m] * carry)
        for c in range(CHUNKS):
            tap_buf[c * part : (c + 1) * part, :] = jnp.exp(-par_buf[c, r, 0, :, local])
        decays = [jnp.broadcast_to(tap_buf[m : m + 1, :], full) for m in range(modes)]
        for j in range(steps):
            at = pl.ds(j, SUB, stride=steps)
            y_buf[slot, at, :] = y_buf[slot, at, :] + tree_sum(terms)
            if j + 1 < steps:
                terms = [terms[m] * decays[m] for m in range(modes)]
        skip = jnp.broadcast_to(skip_ref[:, cols], (2 * SUB, LANES))
        for n in range(rows // (2 * SUB)):
            at = slice(n * 2 * SUB, (n + 1) * 2 * SUB)
            gate = gating_ref[at, cols].astype(jnp.float32)
            out_buf[at, cols] = (
                gate * (y_buf[slot, at, :] + skip * x_buf[slot, at, :])
            ).astype(jnp.bfloat16)

    def sweep(low, high, body):
        @pl.loop(low * tiles, high * tiles)
        def _(i):
            body(i // tiles, i % tiles)

    def end_slot(c, r):
        @pl.loop(0, tiles)
        def _(tile):
            end_states(c, r, tile)

    def widen(r):
        @pl.loop(0, tiles)
        def _(tile):
            cols, local = place(r, tile)
            x_buf[r * tiles + tile] = signal_ref[:, cols].astype(jnp.float32)

    loads[2].wait()
    widen(0)
    for c in range(CHUNKS):
        end_slot(c, 0)

    def relay(c, r):
        par_copy(c, r).wait_recv()
        par_core(c, r).start()

    relay(0, 1)
    for c in range(CHUNKS):
        @pl.loop(1, inner)
        def _(r):
            @pl.when(r + 1 < inner)
            def _():
                relay(c, r + 1)

            if c + 1 < CHUNKS:
                @pl.when(r + 1 == inner)
                def _():
                    relay(c + 1, 1)

            if c == 0:
                widen(r)
            par_core(c, r).wait_recv()
            end_slot(c, r)
            state_copy(c, r).start()

    nothing = jnp.zeros((part, width), jnp.float32)

    def gather_total(c):
        @pl.loop(1, inner)
        def _(r):
            state_copy(c, r).wait_recv()

        state_got[c, 0] = state_out[c, 0]
        decay_block = jnp.exp(par_buf[c, 0, 0] * (-float(rows)))

        def advance(b, run):
            at = wrap(b - me, inner)
            carry_out[c, at] = run
            return decay_block * run + state_got[c, at]

        total_buf[c, 0] = lax.fori_loop(0, inner, advance, nothing)

        @pl.loop(1, groups)
        def _(r):
            total_copy(c, r).start()

    def give_carries(c):
        @pl.loop(1, groups)
        def _(r):
            total_copy(c, r).wait_recv()

        rates = par_buf[c, 0, 0]
        decay_group = jnp.exp(rates * (-float(rows * inner)))

        def join(b, run):
            got = total_buf[c, wrap(block - b, groups)]
            return jnp.where(b < block, decay_group * run + got, run)

        before = lax.fori_loop(0, groups, join, nothing)

        @pl.loop(0, inner)
        def _(r):
            b = wrap(me + r, inner)
            reach = (b * (-rows)).astype(jnp.float32)
            carry_out[c, r] = carry_out[c, r] + jnp.exp(rates * reach) * before

            @pl.when(r > 0)
            def _():
                carry_copy(c, r).start()

        carry_got[c, 0] = carry_out[c, 0]

    cuts = [0, inner // 4, inner // 2, (3 * inner) // 4, inner]
    gather_total(0)
    sweep(cuts[0], cuts[1], within)
    for c in range(1, CHUNKS):
        gather_total(c)
    sweep(cuts[1], cuts[2], within)
    give_carries(0)
    for c in range(1, CHUNKS):
        give_carries(c)
    sweep(cuts[2], cuts[4], within)
    loads[3].wait()
    loads[4].wait()

    @pl.loop(0, inner)
    def _(r):
        @pl.when(r > 0)
        def _():
            for c in range(CHUNKS):
                carry_copy(c, r).wait_recv()

        @pl.loop(0, tiles)
        def _(tile):
            finish(r, tile)

        out_copy(r).start()

    for c in range(CHUNKS):
        @pl.loop(1, inner)
        def _(r):
            par_copy(c, r).wait_send()
            par_core(c, r).wait_send()
            state_copy(c, r).wait_send()
            carry_copy(c, r).wait_send()

        @pl.loop(1, groups)
        def _(r):
            total_copy(c, r).wait_send()

    @pl.loop(0, inner)
    def _(r):
        out_copy(r).wait()


def per_device(signal, gating, decay_rate, residues, skip_gain):
    groups = lax.axis_size("outer")
    inner = lax.axis_size("inner")
    rows, channels = signal.shape
    width, modes = decay_rate.shape
    tiles = width // LANES
    f32 = jnp.float32
    dma = pltpu.SemaphoreType.DMA

    part = modes // CHUNKS

    def states(count):
        return pltpu.VMEM((CHUNKS, count, part, width), f32)

    return pl.pallas_call(
        functools.partial(kernel, groups, inner, modes),
        out_shape=jax.ShapeDtypeStruct((rows, channels), jnp.bfloat16),
        in_specs=[pl.BlockSpec(memory_space=pltpu.HBM)] * 5,
        out_specs=pl.BlockSpec(memory_space=pltpu.HBM),
        scratch_shapes=[
            pltpu.VMEM((modes, width), f32),
            pltpu.VMEM((modes, width), f32),
            pltpu.VMEM((rows, channels), jnp.bfloat16),
            pltpu.VMEM((rows, channels), jnp.bfloat16),
            pltpu.VMEM((1, channels), f32),
            pltpu.VMEM((rows, channels), jnp.bfloat16),
            pltpu.VMEM((CHUNKS, inner, 2, part, width), f32),
            pltpu.VMEM((inner * tiles, rows, LANES), f32),
            pltpu.VMEM((inner * tiles, rows, LANES), f32),
            pltpu.VMEM((inner * tiles, modes, SUB, LANES), f32),
            pltpu.VMEM((inner * tiles, modes, SUB, LANES), f32),
            states(inner), states(inner), states(inner), states(inner), states(groups),
            pltpu.VMEM((4 * modes, LANES), f32),
            dma((5,)), dma((inner,)),
            *[dma((CHUNKS, inner)) for _ in range(8)],
            dma((CHUNKS, groups)), dma((CHUNKS, groups)),
        ],
        compiler_params=pltpu.CompilerParams(
            collective_id=0, has_side_effects=True, vmem_limit_bytes=63 * 1024 * 1024
        ),
        name="modal_scan",
    )(decay_rate.T, residues.T, signal, gating, skip_gain[None, :])


def solution(mesh):
    return jax.shard_map(
        per_device,
        mesh=mesh,
        in_specs=(
            P(("outer", "inner"), None),
            P(("outer", "inner"), None),
            P("inner", None),
            P("inner", None),
            P(),
        ),
        out_specs=P(("outer", "inner"), None),
        check_vma=False,
    )
```

time: 35.6 us -> 35.1 us (0.986)
  Pallas kernels: 33.1 us -> 32.6 us
    pallas_call x1, Pallas kernels: 33.1 us -> 32.6 us  [per_device(): pl.pallas_call(functools.partial(kernel, groups, inner, modes), out_shape...]
where the time goes in v3:
time: 35.1 us; the launch traced here: 34.9 us
  Pallas kernels  32.6 us (93%)
  local copies, waits for them, and re-layouts  2.29 us (7%)
    pallas_call x1, Pallas kernels, per_device(): pl.pallas_call(functools.partial(kernel, groups, inner, modes), out_shape...  32.6 us
    unnamed x1, local copies, waits for them, and re-layouts  2.29 us

profile of v3, /device:TPU:0, one launch (start us, length us, event | category | flops | bytes accessed | tf_op | source)
XLA Modules:
  0.0 34.9 jit_solution(15644197785381091614)
XLA Ops:
  0.0 32.6 %modal_scan.1 = bf16[128,4096]{1,0:T(8,128)(2,1)} custom-call(f32[16,512]{1,0:T(8,128)} %bitcast.3, f32[16,512]{1,0:T(8,128)} %bitcast.4, bf16[128,4096]{1,0:T(8,128)(2,1)} %signal_hbm.1, bf16[128,4096]{1,0:T(8,128)(2,1)} %gating_hbm.1, f32[1,4096]{1,0:T(1,128)} %bitcast.5), custom_call_target="tpu_custom_call" | custom-call | tf_op jit(solution)/shard_map/modal_scan/pallas_call | solution.py:373
  32.6 2.3 %copy.7 = bf16[128,4096]{1,0:T(8,128)(2,1)} copy(bf16[128,4096]{1,0:T(8,128)(2,1)} %modal_scan.1) | data formatting | bytes 2097152

commit v4 on v3

--- a/solution.py
+++ b/solution.py
@@ -131,10 +131,13 @@
         par_buf[c, 0, 1] = residue_ref[at] * jnp.sqrt(one_minus_exp(2.0 * rate_ref[at]))
     pl.semaphore_wait(barrier, inner + groups - 2)
 
+    def order(k):
+        return (k + 1) // 2 + (1 - k % 2) * (inner - k)
+
     for c in range(CHUNKS):
         @pl.loop(1, inner)
         def _(r):
-            par_copy(c, r).start()
+            par_copy(c, order(r)).start()
 
     def place(slot, tile):
         start = wrap(me - slot, inner) * width + tile * LANES
@@ -253,18 +256,19 @@
         def _(r):
             @pl.when(r + 1 < inner)
             def _():
-                relay(c, r + 1)
+                relay(c, order(r + 1))
 
             if c + 1 < CHUNKS:
                 @pl.when(r + 1 == inner)
                 def _():
                     relay(c + 1, 1)
 
+            at = order(r)
             if c == 0:
-                widen(r)
-            par_core(c, r).wait_recv()
-            end_slot(c, r)
-            state_copy(c, r).start()
+                widen(at)
+            par_core(c, at).wait_recv()
+            end_slot(c, at)
+            state_copy(c, at).start()
 
     nothing = jnp.zeros((part, width), jnp.float32)
 

time: 35.1 us -> 36.2 us (1.031)
  Pallas kernels: 32.6 us -> 33.7 us
    pallas_call x1, Pallas kernels: 32.6 us -> 33.7 us  [per_device(): pl.pallas_call(functools.partial(kernel, groups, inner, modes), out_shape...]
where the time goes in v4:
time: 36.2 us; the launch traced here: 36 us
  Pallas kernels  33.7 us (93%)
  local copies, waits for them, and re-layouts  2.29 us (6%)
    pallas_call x1, Pallas kernels, per_device(): pl.pallas_call(functools.partial(kernel, groups, inner, modes), out_shape...  33.7 us
    unnamed x1, local copies, waits for them, and re-layouts  2.29 us

profile of v4, /device:TPU:0, one launch (start us, length us, event | category | flops | bytes accessed | tf_op | source)
XLA Modules:
  0.0 36.0 jit_solution(13955085897886759732)
XLA Ops:
  0.0 33.7 %modal_scan.1 = bf16[128,4096]{1,0:T(8,128)(2,1)} custom-call(f32[16,512]{1,0:T(8,128)} %bitcast.3, f32[16,512]{1,0:T(8,128)} %bitcast.4, bf16[128,4096]{1,0:T(8,128)(2,1)} %signal_hbm.1, bf16[128,4096]{1,0:T(8,128)(2,1)} %gating_hbm.1, f32[1,4096]{1,0:T(1,128)} %bitcast.5), custom_call_target="tpu_custom_call" | custom-call | tf_op jit(solution)/shard_map/modal_scan/pallas_call | solution.py:377
  33.8 2.3 %copy.7 = bf16[128,4096]{1,0:T(8,128)(2,1)} copy(bf16[128,4096]{1,0:T(8,128)(2,1)} %modal_scan.1) | data formatting | bytes 2097152
